TPU v7x, 32 devices: a whole 2x2x4 slice. The times are simulated.
32 devices in a mesh: region: 4 (over x, core), tile: 8 (over z, y).
Axes of the slice: x: 2, y: 2, z: 4, core: 2. Of those that a mesh axis runs over, the one named last changes fastest.
Arguments:
- quantized: bfloat16 [131072, 1024], P(('region', 'tile')), may hold values from -6 to 6
- block_scales: float32 [8, 131072], P(None, ('region', 'tile')), may hold values from 0.25 to 4
- band_width: int32 [32], replicated, may hold values from 1 to 256, as said below
- valid_count: int32 [32], P(('region', 'tile')), may hold values from 1024 to 4096, as said below
- prior_basis: float32 [1024, 64], replicated, may hold values from -0.1875 to 0.1875
Outputs:
- projected: float32 [64, 131072], P(None, ('region', 'tile'))
- new_basis: float32 [1024, 64], replicated
Inputs may be any that keep to these rules, and one draw needn't show every extreme that they name: `band_width`: some tile other than the first of its region has width 256 in every draw. `valid_count`: the last tile's count is 4096 in every draw.
All inputs are finite; a program needn't handle non-finite values.
Results may differ from a plain program's by a relative error of at most 0.0016.
Values may be sent and summed in bfloat16 or wider, within the bound.
A program may use at most 128 MiB of HBM per device.

v0:
```python
import jax
import jax.numpy as jnp
from jax import lax
from jax.sharding import PartitionSpec as P

BAND = 256


def padded_2(cells, sides, width):
    for axis, dim in sides:
        count = lax.axis_size(axis)
        ends = count - 1
        head = lax.slice_in_dim(cells, 0, width, axis=dim)
        tail = lax.slice_in_dim(cells, cells.shape[dim] - width, cells.shape[dim], axis=dim)
        cells = jnp.concatenate(
            [
                lax.ppermute(tail, axis, [(i, (i + 1) % count) for i in range(ends)]),
                cells,
                lax.ppermute(head, axis, [((i + 1) % count, i) for i in range(ends)]),
            ],
            axis=dim,
        )
    return cells


def dequantize(quantized, block_scales):
    tok_rows, feat_dim = quantized.shape
    groups = block_scales.shape[0]
    blocks = (
        quantized.astype(jnp.float32).reshape(tok_rows, groups, feat_dim // groups)
        * block_scales.T[:, :, None]
    )
    return blocks.reshape(tok_rows, feat_dim).astype(jnp.bfloat16)


def blend(initial, neighbour, chosen):
    summed = (initial.astype(jnp.float32) + neighbour.astype(jnp.float32)) * 0.5
    return jnp.where(chosen[:, None], summed, initial.astype(jnp.float32)).astype(jnp.bfloat16)


def finish(update, cross_sum, centred, spread):
    factor = jnp.linalg.cholesky(cross_sum)
    own_basis = jax.scipy.linalg.solve_triangular(factor, update.T, lower=True).T
    new_basis = spread(own_basis)
    projected = lax.dot_general(
        new_basis, centred, (((0,), (1,)), ((), ())), precision=lax.Precision.HIGHEST
    )
    return (projected, new_basis)


def per_device(quantized, block_scales, band_width, valid_count, prior_basis):
    tok_rows, feat_dim = quantized.shape
    n_region = lax.axis_size("region")
    n_tile = lax.axis_size("tile")
    devices = n_region * n_tile
    region_index = lax.axis_index("region")
    tile_index = lax.axis_index("tile")
    tile_number = region_index * n_tile + tile_index
    restored = dequantize(quantized, block_scales)
    padded = padded_2(restored, (("tile", 0),), BAND)
    prev_tail = padded[:BAND]
    next_head = padded[tok_rows + BAND :]
    left_width = jnp.where(tile_index > 0, band_width[tile_number], 0)
    right_width = jnp.where(
        tile_index < n_tile - 1, band_width[jnp.minimum(tile_number + 1, devices - 1)], 0
    )
    positions = jnp.arange(BAND)
    blank = jnp.zeros((BAND, feat_dim), jnp.bfloat16)
    left_part = lax.dynamic_slice_in_dim(
        jnp.concatenate([prev_tail, blank], 0), BAND - left_width, BAND, 0
    )
    right_part = lax.dynamic_slice_in_dim(
        jnp.concatenate([blank, next_head], 0), right_width, BAND, 0
    )
    new_head = blend(restored[:BAND], left_part, positions < left_width)
    new_tail = blend(restored[tok_rows - BAND :], right_part, positions >= BAND - right_width)
    blended = jnp.concatenate([new_head, restored[BAND : tok_rows - BAND], new_tail], 0)
    usable = jnp.arange(tok_rows) < valid_count[0]
    masked = jnp.where(usable[:, None], blended, jnp.zeros((), jnp.bfloat16))
    indicator = jnp.ones((tok_rows,), jnp.bfloat16)
    local_sums = jnp.dot(indicator, masked, preferred_element_type=jnp.float32)
    local_count = valid_count[0].astype(jnp.float32)
    masked_wide = masked.astype(jnp.float32)
    reduced = jnp.dot(masked_wide, prior_basis, precision=lax.Precision.HIGHEST)
    local_update = lax.dot_general(
        masked_wide, reduced, (((0,), (0,)), ((), ())), precision=lax.Precision.HIGHEST
    )
    summed_update, feature_sums, token_count = lax.psum(
        (local_update, local_sums, local_count), ("region", "tile")
    )
    average = feature_sums / token_count
    mean_image = jnp.dot(average, prior_basis, precision=lax.Precision.HIGHEST)
    update = summed_update - jnp.outer(feature_sums, mean_image)
    centred = jnp.where(usable[:, None], masked_wide - average, 0.0)
    cross_sum = jnp.dot(update.T, update, precision=lax.Precision.HIGHEST)
    return finish(update, cross_sum, centred, lambda block: block)


def solution(mesh):
    return jax.shard_map(
        per_device,
        mesh=mesh,
        in_specs=(
            P(("region", "tile"), None),
            P(None, ("region", "tile")),
            P(),
            P(("region", "tile")),
            P(),
        ),
        out_specs=(P(None, ("region", "tile")), P()),
        check_vma=False,
    )
```

profile of v0, /device:TPU:0, one launch (start us, length us, event | category | flops | bytes accessed | tf_op | source)
XLA Modules:
  0.0 243.6 jit_solution(15910361438467005526)
XLA Ops:
  7.2 1.5 copy.7
  8.8 4.6 %mul.34 = f32[4096,8,128]{2,1,0:T(8,128)S(1)} broadcast(f32[4096,8]{1,0:T(8,128)S(1)} %copy.7), dimensions={0,1} | broadcast | bytes 16908288 | tf_op jit(solution)/shard_map/mul | solution.py:30
  13.4 7.7 %fusion = bf16[4096,1024]{1,0:T(8,128)(2,1)S(1)} fusion(f32[512,8,8,128]{3,2,1,0:T(8,128)S(1)} %bitcast.33, bf16[4096,1024]{1,0:T(8,128)(2,1)} %param.5), kind=kLoop, calls=%fused_computation.1 | loop fusion | flops 12582912 | bytes 33554432 | tf_op jit(solution)/shard_map/convert_element_type | solution.py:33
  21.1 3.2 %copy-done.2 = bf16[4096,1024]{1,0:T(8,128)(2,1)} copy-done((bf16[4096,1024]{1,0:T(8,128)(2,1)}, bf16[4096,1024]{1,0:T(8,128)(2,1)S(1)}, u32[]{:S(2)}) %copy-start.2) | copy-done | bytes 8388632
  24.4 4.9 %collective-permute-start = (bf16[256,1024]{1,0:T(8,128)(2,1)S(1)}, bf16[256,1024]{1,0:T(8,128)(2,1)S(1)}, u32[]{:S(2)}, u32[]{:S(2)}) collective-permute-start(bf16[256,1024]{1,0:T(8,128)(2,1)S(1)} %get-tuple-element.6), channel_id=1, source_target_pairs={{0,1},{1,2},{2,3},{3,4},{4,5},{5,6},{6,7},{8,9},{9,10},{10,11},{11... | collective-permute-start | bytes 1572872 | tf_op jit(solution)/shard_map/ppermute | solution.py:17
  29.3 1.3 collective-permute-start.1
  30.7 6.9 %slice.28 = bf16[3584,1024]{1,0:T(8,128)(2,1)} slice(bf16[4096,1024]{1,0:T(8,128)(2,1)} %copy-done.2), slice={[256:3840], [0:1024]} | slice | bytes 14680064 | tf_op jit(solution)/shard_map/slice | solution.py:77
  37.6 0.6 fusion.26
  40.2 11.5 %collective-permute-done = bf16[256,1024]{1,0:T(8,128)(2,1)S(1)} collective-permute-done((bf16[256,1024]{1,0:T(8,128)(2,1)S(1)}, bf16[256,1024]{1,0:T(8,128)(2,1)S(1)}, u32[]{:S(2)}, u32[]{:S(2)}) %collective-permute-start) | collective-permute-done | bytes 524320 | tf_op jit(solution)/shard_map/ppermute | solution.py:17
  51.7 1.8 fusion.9
  53.6 6.2 %maximum_select_fusion = bf16[4096,1024]{1,0:T(8,128)(2,1)S(1)} fusion(bf16[256,1024]{1,0:T(8,128)(2,1)S(1)} %get-tuple-element.5, bf16[3584,1024]{1,0:T(8,128)(2,1)} %slice.28, bf16[256,1024]{1,0:T(8,128)(2,1)S(1)} %get-tuple-element.4, pred[4096]{0:T(1024)(128)(4,1)S(1)} %iota_compare_fusion.2), kind=kLoop, calls=%fused_computation.6 | loop fusion | flops 29360128 | bytes 16781312 | tf_op jit(solution)/shard_map/jit(_where)/select_n | solution.py:79
  59.8 1.2 fusion.21
  61.0 6.7 %fusion.27 = f32[4096,64]{1,0:T(8,128)S(1)} fusion(bf16[4096,1024]{1,0:T(8,128)(2,1)S(1)} %maximum_select_fusion, f32[1024,64]{0,1:T(8,128)S(1)} %copy-done), kind=kOutput, calls=%fused_computation.47 | convolution fusion | flops 3221225472 | bytes 9699328 | tf_op jit(solution)/shard_map/dot_general | solution.py:84
  67.7 5.3 %fusion.28 = f32[1024,64]{0,1:T(8,128)} fusion(bf16[4096,1024]{1,0:T(8,128)(2,1)S(1)} %maximum_select_fusion, f32[4096,64]{1,0:T(8,128)S(1)} %fusion.27), kind=kOutput, calls=%fused_computation.48 | convolution fusion | flops 3221225472 | bytes 9699328 | tf_op jit(solution)/shard_map/dot_general | solution.py:85
  73.0 41.8 %all-reduce.2 = (f32[1024]{0:T(1024)S(1)}, f32[]{:T(128)}) all-reduce(f32[1024]{0:T(1024)S(1)} %bitcast.37, f32[]{:T(128)S(6)} %convert_element_type.40), channel_id=1, replica_groups=mesh['region'=4,'tile'=8] {'region','tile'}, use_global_device_ids=true, to_apply=%region_1.2 | all-reduce | flops 1025 | bytes 8200 | tf_op jit(solution)/shard_map/psum | solution.py:88
  114.7 0.6 broadcast_divide_fusion
  115.7 86.2 %all-reduce.5.cloned.1.call-done = f32[1024,64]{0,1:T(8,128)} async-done(((f32[1024,64]{0,1:T(8,128)}), f32[1024,64]{0,1:T(8,128)}) %all-reduce.5.cloned.1.call-update) | async-done | bytes 262160 | tf_op jit(solution)/shard_map/psum | solution.py:88
  201.9 1.5 fusion.13
  203.4 5.8 %cholesky.16 = f32[64,64]{1,0:T(8,128)S(1)} custom-call(f32[64,64]{1,0:T(8,128)S(1)} %fusion.20), custom_call_target="Cholesky" | custom-call | tf_op jit(solution)/shard_map/jit(cholesky)/cholesky | solution.py:42
  209.3 0.6 compare_reduce_fusion
  210.0 0.7 fusion.18
  210.6 4.9 %custom-call.7 = f32[1,64,64]{1,2,0:T(8,128)S(1)} custom-call(f32[1,64,64]{2,1,0:T(8,128)S(1)} %fusion.18), custom_call_target="InvertDiagBlocksLowerTriangular" | custom-call | tf_op jit(solution)/shard_map/jit(_solve_triangular)/triangular_solve | solution.py:43
  215.5 1.4 fusion.12
  217.0 19.8 %fusion.1 = f32[64,4096]{1,0:T(8,128)} fusion(f32[64,1024]{1,0:T(8,128)S(1)} %fusion.12, bf16[4096,1024]{1,0:T(8,128)(2,1)} %copy-done.1, f32[1024]{0:T(1024)S(1)} %broadcast_divide_fusion, pred[4096]{0:T(1024)(128)(4,1)S(1)} %iota_compare_fusion.2), kind=kOutput, calls=%fused_computation.2 | convolution fusion | flops 3233808384 | bytes 9707520 | tf_op jit(solution)/shard_map/dot_general | solution.py:45
  (19 shorter events, 0.5 us)
Async XLA Ops:
  7.2 53.9 %copy-start = (f32[1024,64]{0,1:T(8,128)S(1)}, f32[1024,64]{0,1:T(8,128)}, u32[]{:S(2)}) copy-start(f32[1024,64]{0,1:T(8,128)} %param.9) | copy-start | bytes 786436
  7.2 194.7 %all-reduce.5.cloned.1.call-start = ((), (), s32[]{:S(2)}) async-start(), calls=%async_computation | async-start | bytes 524288 | tf_op jit(solution)/shard_map/psum | solution.py:88
  21.1 3.2 %copy-start.2 = (bf16[4096,1024]{1,0:T(8,128)(2,1)}, bf16[4096,1024]{1,0:T(8,128)(2,1)S(1)}, u32[]{:S(2)}) copy-start(bf16[4096,1024]{1,0:T(8,128)(2,1)S(1)} %fusion) | copy-start | bytes 25165828
  24.3 13.3 %copy-start.4 = (s32[32]{0:T(128)S(1)}, s32[32]{0:T(128)}, u32[]{:S(2)}) copy-start(s32[32]{0:T(128)} %param.7) | copy-start | bytes 388
  24.4 27.3 %collective-permute-start = (bf16[256,1024]{1,0:T(8,128)(2,1)S(1)}, bf16[256,1024]{1,0:T(8,128)(2,1)S(1)}, u32[]{:S(2)}, u32[]{:S(2)}) collective-permute-start(bf16[256,1024]{1,0:T(8,128)(2,1)S(1)} %get-tuple-element.6), channel_id=1, source_target_pairs={{0,1},{1,2},{2,3},{3,4},{4,5},{5,6},{6,7},{8,9},{9,10},{10,11},{11... | collective-permute-start | bytes 1572872 | tf_op jit(solution)/shard_map/ppermute | solution.py:17
  29.3 22.4 %collective-permute-start.1 = (bf16[256,1024]{1,0:T(8,128)(2,1)S(1)}, bf16[256,1024]{1,0:T(8,128)(2,1)S(1)}, u32[]{:S(2)}, u32[]{:S(2)}) collective-permute-start(bf16[256,1024]{1,0:T(8,128)(2,1)S(1)} %get-tuple-element.7), channel_id=1, source_target_pairs={{1,0},{2,1},{3,2},{4,3},{5,4},{6,5},{7,6},{9,8},{10,9},{11,10},{12... | collective-permute-start | bytes 1572872 | tf_op jit(solution)/shard_map/ppermute | solution.py:19
  59.8 7.9 %copy-start.1 = (bf16[4096,1024]{1,0:T(8,128)(2,1)}, bf16[4096,1024]{1,0:T(8,128)(2,1)S(1)}, u32[]{:S(2)}) copy-start(bf16[4096,1024]{1,0:T(8,128)(2,1)S(1)} %maximum_select_fusion) | copy-start | bytes 25165828
  216.9 19.8 %copy-start.3 = (f32[64,1024]{1,0:T(8,128)}, f32[64,1024]{1,0:T(8,128)S(1)}, u32[]{:S(2)}) copy-start(f32[64,1024]{1,0:T(8,128)S(1)} %fusion.12) | copy-start | bytes 786436
Sparse Core Ops, SparseCore 0:
  73.1 128.7 all-reduce.4
where the time goes:
time: 244 us
  waiting for transfers between devices  97.8 us (40%)
  blocking collectives  41.8 us (17%)
  matrix products  36.1 us (15%)
  other arithmetic  28.6 us (12%)
  local copies, waits for them, and re-layouts  17 us (7%)
  between operations  16.2 us (7%)
  starting transfers between devices  6.26 us (3%)
    psum x1, waiting for transfers between devices, per_device(): lax.psum((local_update, local_sums, local_count), ('region', 'tile'))  86.2 us
    psum x1, blocking collectives, per_device(): lax.psum((local_update, local_sums, local_count), ('region', 'tile'))  41.8 us
    dot_general x1, matrix products, finish(): lax.dot_general(new_basis, centred, (((0,), (1,)), ((), ())), precision=l...  19.8 us
    ppermute x1, waiting for transfers between devices, padded_2(): lax.ppermute(tail, axis, [(i, (i + 1) % count) for i in range(ends)])  11.5 us
    convert_element_type x1, other arithmetic, dequantize(): return blocks.reshape(tok_rows, feat_dim).astype(jnp.bfloat16)  7.73 us
    slice x1, local copies, waits for them, and re-layouts, per_device(): restored[BAND:tok_rows - BAND]  6.93 us
    dot_general x1, matrix products, per_device(): reduced = jnp.dot(masked_wide, prior_basis, precision=lax.Precision.HIGHEST)  6.67 us
    another operation x3, other arithmetic, finish(): factor = jnp.linalg.cholesky(cross_sum)  6.52 us
  transfers between devices with their start and end apart: 3, of which 2 were waited for; matrix products, arithmetic and copies ran while one was open for 3% of the time, Pallas kernels for 0%

commit v1 on v0

--- a/solution.py
+++ b/solution.py
@@ -86,7 +86,7 @@
         masked_wide, reduced, (((0,), (0,)), ((), ())), precision=lax.Precision.HIGHEST
     )
     summed_update, feature_sums, token_count = lax.psum(
-        (local_update, local_sums, local_count), ("region", "tile")
+        lax.psum((local_update, local_sums, local_count), axis_name="tile"), "region"
     )
     average = feature_sums / token_count
     mean_image = jnp.dot(average, prior_basis, precision=lax.Precision.HIGHEST)

time: 244 us -> 221 us (0.906)
  waiting for transfers between devices: 97.8 us -> 83.8 us
  blocking collectives: 41.8 us -> 29.2 us
  matrix products: 36.1 us -> 39.4 us
    psum x1 -> x2, waiting for transfers between devices: 86.2 us -> 72.2 us  [the longest x1 39.3 us: per_device(): lax.psum((local_update, local_sums, local_count), axis_name='tile')]
    psum x1 -> x2, blocking collectives: 41.8 us -> 29.2 us  [the longest x1 22.4 us: per_device(): lax.psum((local_update, local_sums, local_count), axis_name='tile')]
    dot_general x1, matrix products: 1.19 us -> 4.57 us  [per_device(): local_sums = jnp.dot(indicator, masked, preferred_element_type=jnp.float32)]
  transfers between devices with their start and end apart: 3 -> 4, of which waited for: 2 -> 3; matrix products, arithmetic and copies ran while one was open for 3% -> 6% of each run, Pallas kernels for 0% -> 0%
where the time goes in v1:
time: 221 us
  waiting for transfers between devices  83.8 us (38%)
  matrix products  39.4 us (18%)
  blocking collectives  29.2 us (13%)
  other arithmetic  28.6 us (13%)
  local copies, waits for them, and re-layouts  17 us (8%)
  between operations  16.2 us (7%)
  starting transfers between devices  6.52 us (3%)
    psum x1, waiting for transfers between devices, per_device(): lax.psum((local_update, local_sums, local_count), axis_name='tile')  39.3 us
    psum x1, waiting for transfers between devices, per_device(): lax.psum(lax.psum((local_update, local_sums, local_count), axis_name='til...  32.9 us
    psum x1, blocking collectives, per_device(): lax.psum((local_update, local_sums, local_count), axis_name='tile')  22.4 us
    dot_general x1, matrix products, finish(): lax.dot_general(new_basis, centred, (((0,), (1,)), ((), ())), precision=l...  19.8 us
    ppermute x1, waiting for transfers between devices, padded_2(): lax.ppermute(tail, axis, [(i, (i + 1) % count) for i in range(ends)])  11.5 us
    convert_element_type x1, other arithmetic, dequantize(): return blocks.reshape(tok_rows, feat_dim).astype(jnp.bfloat16)  7.73 us
    slice x1, local copies, waits for them, and re-layouts, per_device(): restored[BAND:tok_rows - BAND]  6.94 us
    psum x1, blocking collectives, per_device(): lax.psum(lax.psum((local_update, local_sums, local_count), axis_name='til...  6.77 us
  transfers between devices with their start and end apart: 4, of which 3 were waited for; matrix products, arithmetic and copies ran while one was open for 6% of the time, Pallas kernels for 0%

profile of v1, /device:TPU:0, one launch (start us, length us, event | category | flops | bytes accessed | tf_op | source)
XLA Modules:
  0.0 220.7 jit_solution(13792028329443223035)
XLA Ops:
  7.2 1.5 copy.7
  8.8 4.6 %mul.34 = f32[4096,8,128]{2,1,0:T(8,128)S(1)} broadcast(f32[4096,8]{1,0:T(8,128)S(1)} %copy.7), dimensions={0,1} | broadcast | bytes 16908288 | tf_op jit(solution)/shard_map/mul | solution.py:30
  13.4 7.7 %fusion = bf16[4096,1024]{1,0:T(8,128)(2,1)S(1)} fusion(f32[512,8,8,128]{3,2,1,0:T(8,128)S(1)} %bitcast.33, bf16[4096,1024]{1,0:T(8,128)(2,1)} %param.5), kind=kLoop, calls=%fused_computation.1 | loop fusion | flops 12582912 | bytes 33554432 | tf_op jit(solution)/shard_map/convert_element_type | solution.py:33
  21.1 3.2 %copy-done.2 = bf16[4096,1024]{1,0:T(8,128)(2,1)} copy-done((bf16[4096,1024]{1,0:T(8,128)(2,1)}, bf16[4096,1024]{1,0:T(8,128)(2,1)S(1)}, u32[]{:S(2)}) %copy-start.2) | copy-done | bytes 8388632
  24.4 4.9 %collective-permute-start = (bf16[256,1024]{1,0:T(8,128)(2,1)S(1)}, bf16[256,1024]{1,0:T(8,128)(2,1)S(1)}, u32[]{:S(2)}, u32[]{:S(2)}) collective-permute-start(bf16[256,1024]{1,0:T(8,128)(2,1)S(1)} %get-tuple-element.8), channel_id=1, source_target_pairs={{0,1},{1,2},{2,3},{3,4},{4,5},{5,6},{6,7},{8,9},{9,10},{10,11},{11... | collective-permute-start | bytes 1572872 | tf_op jit(solution)/shard_map/ppermute | solution.py:17
  29.3 1.3 collective-permute-start.1
  30.7 6.9 %slice.28 = bf16[3584,1024]{1,0:T(8,128)(2,1)} slice(bf16[4096,1024]{1,0:T(8,128)(2,1)} %copy-done.2), slice={[256:3840], [0:1024]} | slice | bytes 14680064 | tf_op jit(solution)/shard_map/slice | solution.py:77
  40.2 11.5 %collective-permute-done = bf16[256,1024]{1,0:T(8,128)(2,1)S(1)} collective-permute-done((bf16[256,1024]{1,0:T(8,128)(2,1)S(1)}, bf16[256,1024]{1,0:T(8,128)(2,1)S(1)}, u32[]{:S(2)}, u32[]{:S(2)}) %collective-permute-start) | collective-permute-done | bytes 524320 | tf_op jit(solution)/shard_map/ppermute | solution.py:17
  51.7 1.8 fusion.9
  53.6 6.2 %maximum_select_fusion = bf16[4096,1024]{1,0:T(8,128)(2,1)S(1)} fusion(bf16[256,1024]{1,0:T(8,128)(2,1)S(1)} %get-tuple-element.7, bf16[3584,1024]{1,0:T(8,128)(2,1)} %slice.28, bf16[256,1024]{1,0:T(8,128)(2,1)S(1)} %get-tuple-element.6, pred[4096]{0:T(1024)(128)(4,1)S(1)} %iota_compare_fusion.2), kind=kLoop, calls=%fused_computation.6 | loop fusion | flops 29360128 | bytes 16781312 | tf_op jit(solution)/shard_map/jit(_where)/select_n | solution.py:79
  59.8 6.7 %fusion.27 = f32[4096,64]{1,0:T(8,128)S(1)} fusion(bf16[4096,1024]{1,0:T(8,128)(2,1)S(1)} %maximum_select_fusion, f32[1024,64]{0,1:T(8,128)S(1)} %copy-done), kind=kOutput, calls=%fused_computation.47 | convolution fusion | flops 3221225472 | bytes 9699328 | tf_op jit(solution)/shard_map/dot_general | solution.py:84
  66.5 5.3 %fusion.28 = f32[1024,64]{0,1:T(8,128)} fusion(bf16[4096,1024]{1,0:T(8,128)(2,1)S(1)} %maximum_select_fusion, f32[4096,64]{1,0:T(8,128)S(1)} %fusion.27), kind=kOutput, calls=%fused_computation.48 | convolution fusion | flops 3221225472 | bytes 9699328 | tf_op jit(solution)/shard_map/dot_general | solution.py:85
  72.1 4.6 %fusion.21 = f32[1,1024]{1,0:T(1,128)S(1)} fusion(bf16[4096,1024]{1,0:T(8,128)(2,1)} %copy-done.1), kind=kOutput, calls=%fused_computation.37 | convolution fusion | flops 8388608 | bytes 8392704 | tf_op jit(solution)/shard_map/dot_general | solution.py:81
  76.6 22.4 %all-reduce.2 = (f32[1024]{0:T(1024)S(1)}, f32[]{:T(128)}) all-reduce(f32[1024]{0:T(1024)S(1)} %bitcast.37, f32[]{:T(128)S(6)} %convert_element_type.40), channel_id=1, replica_groups=mesh['region'=4,'tile'=8] {'tile'}, use_global_device_ids=true, to_apply=%region_2.3 | all-reduce | flops 1025 | bytes 8200 | tf_op jit(solution)/shard_map/psum | solution.py:89
  99.0 6.8 %all-reduce.3 = (f32[1024]{0:T(1024)S(1)}, f32[]{:T(128)}) all-reduce(f32[1024]{0:T(1024)S(1)} %get-tuple-element.2, f32[]{:T(128)} %get-tuple-element.3), channel_id=1, replica_groups=mesh['region'=4,'tile'=8] {'region'}, use_global_device_ids=true, to_apply=%region_3.4 | all-reduce | flops 1025 | bytes 8200 | tf_op jit(solution)/shard_map/psum | solution.py:88
  105.8 39.3 %all-reduce.7.cloned.1.call-done = f32[1024,64]{0,1:T(8,128)} async-done(((f32[1024,64]{0,1:T(8,128)}), f32[1024,64]{0,1:T(8,128)}) %all-reduce.7.cloned.1.call-update) | async-done | bytes 262160 | tf_op jit(solution)/shard_map/psum | solution.py:89
  145.2 0.7 broadcast_divide_fusion
  146.1 32.9 %all-reduce.9.cloned.1.call-done = f32[1024,64]{0,1:T(8,128)} async-done(((f32[1024,64]{0,1:T(8,128)}), f32[1024,64]{0,1:T(8,128)}) %all-reduce.9.cloned.1.call-update) | async-done | bytes 262160 | tf_op jit(solution)/shard_map/psum | solution.py:88
  179.0 1.5 fusion.13
  180.6 5.8 %cholesky.16 = f32[64,64]{1,0:T(8,128)S(1)} custom-call(f32[64,64]{1,0:T(8,128)S(1)} %fusion.20), custom_call_target="Cholesky" | custom-call | tf_op jit(solution)/shard_map/jit(cholesky)/cholesky | solution.py:42
  187.1 0.7 fusion.18
  187.7 4.9 %custom-call.7 = f32[1,64,64]{1,2,0:T(8,128)S(1)} custom-call(f32[1,64,64]{2,1,0:T(8,128)S(1)} %fusion.18), custom_call_target="InvertDiagBlocksLowerTriangular" | custom-call | tf_op jit(solution)/shard_map/jit(_solve_triangular)/triangular_solve | solution.py:43
  192.6 1.4 fusion.12
  194.1 19.8 %fusion.1 = f32[64,4096]{1,0:T(8,128)} fusion(f32[64,1024]{1,0:T(8,128)S(1)} %fusion.12, bf16[4096,1024]{1,0:T(8,128)(2,1)} %copy-done.1, f32[1024]{0:T(1024)S(1)} %broadcast_divide_fusion, pred[4096]{0:T(1024)(128)(4,1)S(1)} %iota_compare_fusion.2), kind=kOutput, calls=%fused_computation.2 | convolution fusion | flops 3233808384 | bytes 9707520 | tf_op jit(solution)/shard_map/dot_general | solution.py:45
  (23 shorter events, 2.1 us)
Async XLA Ops:
  7.2 52.6 %copy-start = (f32[1024,64]{0,1:T(8,128)S(1)}, f32[1024,64]{0,1:T(8,128)}, u32[]{:S(2)}) copy-start(f32[1024,64]{0,1:T(8,128)} %param.9) | copy-start | bytes 786436
  7.2 138.0 %all-reduce.7.cloned.1.call-start = ((), (), s32[]{:S(2)}) async-start(), calls=%async_computation | async-start | bytes 524288 | tf_op jit(solution)/shard_map/psum | solution.py:89
  21.1 3.2 %copy-start.2 = (bf16[4096,1024]{1,0:T(8,128)(2,1)}, bf16[4096,1024]{1,0:T(8,128)(2,1)S(1)}, u32[]{:S(2)}) copy-start(bf16[4096,1024]{1,0:T(8,128)(2,1)S(1)} %fusion) | copy-start | bytes 25165828
  24.3 13.3 %copy-start.4 = (s32[32]{0:T(128)S(1)}, s32[32]{0:T(128)}, u32[]{:S(2)}) copy-start(s32[32]{0:T(128)} %param.7) | copy-start | bytes 388
  24.4 27.3 %collective-permute-start = (bf16[256,1024]{1,0:T(8,128)(2,1)S(1)}, bf16[256,1024]{1,0:T(8,128)(2,1)S(1)}, u32[]{:S(2)}, u32[]{:S(2)}) collective-permute-start(bf16[256,1024]{1,0:T(8,128)(2,1)S(1)} %get-tuple-element.8), channel_id=1, source_target_pairs={{0,1},{1,2},{2,3},{3,4},{4,5},{5,6},{6,7},{8,9},{9,10},{10,11},{11... | collective-permute-start | bytes 1572872 | tf_op jit(solution)/shard_map/ppermute | solution.py:17
  29.3 22.4 %collective-permute-start.1 = (bf16[256,1024]{1,0:T(8,128)(2,1)S(1)}, bf16[256,1024]{1,0:T(8,128)(2,1)S(1)}, u32[]{:S(2)}, u32[]{:S(2)}) collective-permute-start(bf16[256,1024]{1,0:T(8,128)(2,1)S(1)} %get-tuple-element.9), channel_id=1, source_target_pairs={{1,0},{2,1},{3,2},{4,3},{5,4},{6,5},{7,6},{9,8},{10,9},{11,10},{12... | collective-permute-start | bytes 1572872 | tf_op jit(solution)/shard_map/ppermute | solution.py:19
  59.8 6.7 %copy-start.1 = (bf16[4096,1024]{1,0:T(8,128)(2,1)}, bf16[4096,1024]{1,0:T(8,128)(2,1)S(1)}, u32[]{:S(2)}) copy-start(bf16[4096,1024]{1,0:T(8,128)(2,1)S(1)} %maximum_select_fusion) | copy-start | bytes 25165828
  71.8 107.2 %all-reduce.9.cloned.1.call-start = ((), (), s32[]{:S(2)}) async-start(), calls=%async_computation.1 | async-start | bytes 524288 | tf_op jit(solution)/shard_map/psum | solution.py:88
  194.1 19.8 %copy-start.3 = (f32[64,1024]{1,0:T(8,128)}, f32[64,1024]{1,0:T(8,128)S(1)}, u32[]{:S(2)}) copy-start(f32[64,1024]{1,0:T(8,128)S(1)} %fusion.12) | copy-start | bytes 786436
Sparse Core Ops, SparseCore 0:
  71.9 73.1 all-reduce.6
  147.5 31.4 all-reduce.8
